TPU v7x, 32 devices: a whole 2x2x4 slice. The times are simulated.
32 devices in a mesh: clip: 2 (over x), space: 4 (over y, core), tm: 4 (over z).
Axes of the slice: x: 2, y: 2, z: 4, core: 2. Of those that a mesh axis runs over, the one named last changes fastest.
Arguments:
- block_input: bfloat16 [8, 12, 160, 384], P(('clip', 'tm'), 'space'), parts along dimension 0, may hold values from -24 to 24, as said below
- conv_input: bfloat16 [8, 12, 160, 384], P(('clip', 'tm'), 'space'), parts along dimension 0, may hold values from -24 to 24, as said below
- norm_gain: float32 [384], replicated, may hold values from 0.1 to 1.9
- norm_bias: float32 [384], replicated, may hold values from -3 to 3
- conv_weight: bfloat16 [3, 3, 3, 384, 384], replicated, may hold values from -0.0625 to 0.0625
- conv_bias: float32 [384], replicated, may hold values from -1.5 to 1.5
- attn_gain: float32 [384], replicated, may hold values from 0.1 to 1.9
- attn_bias: float32 [384], replicated, may hold values from -1.5 to 1.5
- query_weight: bfloat16 [384, 384], replicated, may hold values from -4 to 4
- query_bias: float32 [384], replicated, may hold values from -1.5 to 1.5
- key_weight: bfloat16 [384, 384], replicated, may hold values from -4 to 4
- value_weight: bfloat16 [384, 384], replicated, may hold values from -0.3125 to 0.3125
- value_bias: float32 [384], replicated, may hold values from -3 to 3
- out_weight: bfloat16 [384, 384], replicated, may hold values from -0.3125 to 0.3125
- out_bias: float32 [384], replicated, may hold values from -3 to 3
Outputs:
- block_output: bfloat16 [8, 12, 160, 384], P(('clip', 'tm'), 'space'), parts along dimension 0
There are 2 independent parts, one for each index of `clip`. A program takes and returns all parts, laid end to end along the dimension named above; an argument that names none is the same for every part. Nothing has to cross between parts.
Inputs may be any that keep to these rules, and one draw needn't show every extreme that they name: `block_input`: finite activations. `conv_input`: finite activations.
All inputs are finite; a program needn't handle non-finite values.
Results may differ from a plain program's by a relative error of at most 0.0075.
Values may be sent and summed in bfloat16 or wider, within the bound.
No kernel may reach another device: no remote copies, remote signals or barrier semaphores. Data moves between devices by JAX's collectives and lax.ppermute only.
A program may use at most 128 MiB of HBM per device.

v0:
```python
import jax
import jax.numpy as jnp
from jax import lax
from jax.sharding import PartitionSpec as P


def from_behind(value, axis, steps):
    count = lax.axis_size(axis)
    leading, last = (max(0, -steps), min(count, count - steps))
    return lax.ppermute(value, axis, [(source, source + steps) for source in range(leading, last)])


def padded_2(x, sides, width):
    for axis, dim in sides:
        peers, length = (lax.axis_size(axis), x.shape[dim])
        up = [(i, (i + 1) % peers) for i in range(peers - 1)]
        down = [(j, i) for i, j in up]
        last = lax.slice_in_dim(x, length - width, length, axis=dim)
        leading = lax.slice_in_dim(x, 0, width, axis=dim)
        before = lax.ppermute(last, axis, up)
        after = lax.ppermute(leading, axis, down)
        x = jnp.concatenate([before, x, after], axis=dim)
    return x


def rms_norm(field, gain, bias):
    mean_square = jnp.mean(field * field, axis=-1, keepdims=True)
    return field * lax.rsqrt(mean_square + 1e-06) * gain + bias


def causal_conv(padded, conv_weight, frame_count, row_count, columns):
    channels = padded.shape[-1]
    running = jnp.zeros((frame_count * row_count * columns, channels), jnp.float32)
    for tap_t in range(3):
        for tap_y in range(3):
            window = padded[tap_t : tap_t + frame_count, tap_y : tap_y + row_count]
            joined = jnp.concatenate(
                [window[:, :, tap_x : tap_x + columns] for tap_x in range(3)], axis=-1
            )
            joined = joined.reshape(-1, 3 * channels)
            kernel = conv_weight[tap_t, tap_y].reshape(3 * channels, channels)
            running = running + jnp.dot(joined, kernel, preferred_element_type=jnp.float32)
    return running.reshape(frame_count, row_count, columns, channels)


def absorb(state, queries, key_rows, value_rows, score_scale):
    numer_acc, denom_acc, max_acc = state
    scores = (
        jnp.einsum("fqc,fkc->fqk", queries, key_rows, preferred_element_type=jnp.float32)
        * score_scale
    )
    new_max = jnp.maximum(max_acc, jnp.max(scores, axis=-1))
    expd = jnp.exp(scores - new_max[..., None])
    weights = expd.astype(jnp.bfloat16)
    added = jnp.einsum("fqk,fkc->fqc", weights, value_rows, preferred_element_type=jnp.float32)
    numer_acc = added
    denom_acc = jnp.sum(expd, axis=-1)
    return (numer_acc, denom_acc, new_max)


def shards(
    block_input,
    conv_input,
    norm_gain,
    norm_bias,
    conv_weight,
    conv_bias,
    attn_gain,
    attn_bias,
    query_weight,
    query_bias,
    key_weight,
    value_weight,
    value_bias,
    out_weight,
    out_bias,
):
    frame_count, row_count, columns, channels = block_input.shape
    field = conv_input.astype(jnp.float32)
    activated = jax.nn.silu(rms_norm(field, norm_gain, norm_bias)).astype(jnp.bfloat16)
    earlier = [from_behind(activated, "tm", offset) for offset in (1, 2)]
    stacked = jnp.concatenate([earlier[1], earlier[0], activated], axis=0)
    padded = padded_2(stacked, (("space", 1),), 1)
    padded = jnp.pad(padded, ((0, 0), (0, 0), (1, 1), (0, 0)))
    convolved = causal_conv(padded, conv_weight, frame_count, row_count, columns) + conv_bias
    mixed = (block_input.astype(jnp.float32) + convolved).astype(jnp.bfloat16)
    mixed_wide = mixed.astype(jnp.float32)
    normed = rms_norm(mixed_wide, attn_gain, attn_bias).astype(jnp.bfloat16)
    flat_rows = normed.reshape(frame_count, row_count * columns, channels)
    score_scale = float(channels) ** (-0.5)
    queries = (
        jnp.dot(flat_rows, query_weight, preferred_element_type=jnp.float32) + query_bias
    ).astype(jnp.bfloat16)
    query_count = row_count * columns
    start_state = (
        jnp.zeros((frame_count, query_count, channels), jnp.float32),
        jnp.zeros((frame_count, query_count), jnp.float32),
        jnp.full((frame_count, query_count), -1e30, jnp.float32),
    )
    source = lax.all_gather(normed, "space", axis=1, tiled=True).reshape(frame_count, -1, channels)
    key_rows = jnp.dot(source, key_weight, preferred_element_type=jnp.float32).astype(jnp.bfloat16)
    value_rows = (
        jnp.dot(source, value_weight, preferred_element_type=jnp.float32) + value_bias
    ).astype(jnp.bfloat16)
    numer_acc, denom_acc, max_acc = absorb(start_state, queries, key_rows, value_rows, score_scale)
    attended = (numer_acc / denom_acc[..., None]).astype(jnp.bfloat16)
    projected = jnp.dot(attended, out_weight, preferred_element_type=jnp.float32) + out_bias
    return (mixed_wide + projected.reshape(mixed_wide.shape)).astype(jnp.bfloat16)


def solution(mesh):
    placed = (
        P(("clip", "tm"), "space", None, None),
        P(("clip", "tm"), "space", None, None),
        P(),
        P(),
        P(),
        P(),
        P(),
        P(),
        P(),
        P(),
        P(),
        P(),
        P(),
        P(),
        P(),
    )
    return jax.shard_map(
        shards,
        mesh=mesh,
        in_specs=placed,
        out_specs=P(("clip", "tm"), "space", None, None),
        check_vma=False,
    )
```

profile of v0, /device:TPU:0, one launch (start us, length us, event | category | flops | bytes accessed | tf_op | source)
XLA Modules:
  0.0 103.6 jit_solution(10755714841860632833)
XLA Ops:
  6.5 1.2 %fusion.35 = f32[3,160]{1,0:T(4,128)S(1)} fusion(bf16[1,3,160,384]{3,2,1,0:T(8,128)(2,1)} %param.16), kind=kLoop, calls=%fused_computation.72 | loop fusion | flops 552480 | bytes 370560 | tf_op jit(solution)/shard_map/reduce_sum | solution.py:27
  7.8 1.3 %fusion.43 = bf16[1,3,160,384]{3,2,1,0:T(8,128)(2,1)S(1)} fusion(bf16[1,3,160,384]{3,2,1,0:T(8,128)(2,1)} %param.16, f32[384]{0:T(512)} %param.18, f32[384]{0:T(512)} %param.17, f32[3,160]{1,0:T(4,128)S(1)} %add_rsqrt_fusion.1), kind=kLoop, calls=%fused_computation.80 | loop fusion | flops 1658880 | bytes 742272 | tf_op jit(solution)/shard_map/convert_element_type | solution.py:80
  9.1 5.0 %collective-permute-start.1 = (bf16[1,3,160,384]{3,2,1,0:T(8,128)(2,1)S(1)}, bf16[1,3,160,384]{3,2,1,0:T(8,128)(2,1)S(1)}, u32[]{:S(2)}, u32[]{:S(2)}) collective-permute-start(bf16[1,3,160,384]{3,2,1,0:T(8,128)(2,1)S(1)} %fusion.43), channel_id=1, source_target_pairs={{0,1},{1,2},{2,3},{4,5},{5,6},{6,7},{8,9},{9,10},{10,11},{12,13},{... | collective-permute-start | bytes 1105928 | tf_op jit(solution)/shard_map/ppermute | solution.py:10
  14.1 4.5 %collective-permute-start = (bf16[1,3,160,384]{3,2,1,0:T(8,128)(2,1)S(1)}, bf16[1,3,160,384]{3,2,1,0:T(8,128)(2,1)S(1)}, u32[]{:S(2)}, u32[]{:S(2)}) collective-permute-start(bf16[1,3,160,384]{3,2,1,0:T(8,128)(2,1)S(1)} %fusion.43), channel_id=1, source_target_pairs={{0,2},{1,3},{4,6},{5,7},{8,10},{9,11},{12,14},{13,15},{16,18},{17,... | collective-permute-start | bytes 1105928 | tf_op jit(solution)/shard_map/ppermute | solution.py:10
  18.6 4.4 %collective-permute-done.1 = bf16[1,3,160,384]{3,2,1,0:T(8,128)(2,1)S(1)} collective-permute-done((bf16[1,3,160,384]{3,2,1,0:T(8,128)(2,1)S(1)}, bf16[1,3,160,384]{3,2,1,0:T(8,128)(2,1)S(1)}, u32[]{:S(2)}, u32[]{:S(2)}) %collective-permute-start.1) | collective-permute-done | bytes 368672 | tf_op jit(solution)/shard_map/ppermute | solution.py:10
  23.0 6.8 %collective-permute-done = bf16[1,3,160,384]{3,2,1,0:T(8,128)(2,1)S(1)} collective-permute-done((bf16[1,3,160,384]{3,2,1,0:T(8,128)(2,1)S(1)}, bf16[1,3,160,384]{3,2,1,0:T(8,128)(2,1)S(1)}, u32[]{:S(2)}, u32[]{:S(2)}) %collective-permute-start) | collective-permute-done | bytes 368672 | tf_op jit(solution)/shard_map/ppermute | solution.py:10
  29.9 1.3 %collective-permute-start.2 = (bf16[3,1,160,384]{3,2,1,0:T(8,128)(2,1)S(1)}, bf16[3,1,160,384]{3,2,1,0:T(8,128)(2,1)S(1)}, u32[]{:S(2)}, u32[]{:S(2)}) collective-permute-start(bf16[3,1,160,384]{3,2,1,0:T(8,128)(2,1)S(1)} %get-tuple-element.41), channel_id=1, source_target_pairs={{0,4},{4,8},{8,12},{1,5},{5,9},{9,13},{2,6},{6,10},{10,14},{3,7},{... | collective-permute-start | bytes 1105928 | tf_op jit(solution)/shard_map/ppermute | solution.py:20
  31.3 1.3 %collective-permute-start.3 = (bf16[3,1,160,384]{3,2,1,0:T(8,128)(2,1)S(1)}, bf16[3,1,160,384]{3,2,1,0:T(8,128)(2,1)S(1)}, u32[]{:S(2)}, u32[]{:S(2)}) collective-permute-start(bf16[3,1,160,384]{3,2,1,0:T(8,128)(2,1)S(1)} %get-tuple-element.40), channel_id=1, source_target_pairs={{4,0},{8,4},{12,8},{5,1},{9,5},{13,9},{6,2},{10,6},{14,10},{7,3},{... | collective-permute-start | bytes 1105928 | tf_op jit(solution)/shard_map/ppermute | solution.py:21
  32.6 3.9 %fusion.53 = (bf16[1,1,3,384,384]{4,3,2,1,0:T(8,128)(2,1)S(1)}, bf16[1,1,3,384,384]{4,3,2,1,0:T(8,128)(2,1)S(1)}, bf16[1,1,3,384,384]{4,3,2,1,0:T(8,128)(2,1)S(1...) fusion(bf16[3,3,3,384,384]{4,3,2,1,0:T(8,128)(2,1)} %param.19), kind=kLoop, calls=%fused_computation.96 | loop fusion | bytes 15925248 | tf_op jit(solution)/shard_map/slice | solution.py:41
  36.6 1.5 %select_maximum_fusion = bf16[3,5,162,384]{3,2,1,0:T(8,128)(2,1)S(1)} fusion(bf16[3,1,160,384]{3,2,1,0:T(8,128)(2,1)S(1)} %collective-permute-done.3, bf16[3,1,160,384]{3,2,1,0:T(8,128)(2,1)S(1)} %collective-permute-done.2, bf16[1,3,160,384]{3,2,1,0:T(8,128)(2,1)S(1)} %fusion.43, bf16[1,3,160,384]{3,2,1,0:T(8,128)(2,1)S(1)} %collective-permute-done.1, ...), kind=kLoop, calls=%fused_computation.10 | loop fusion | flops 16796160 | bytes 3709440 | tf_op jit(solution)/shard_map/concatenate | solution.py:22
  38.1 1.1 %fusion.54 = (bf16[1,3,160,384]{3,2,1,0:T(8,128)(2,1)S(1)}, bf16[1,3,160,384]{3,2,1,0:T(8,128)(2,1)S(1)}, bf16[1,3,160,384]{3,2,1,0:T(8,128)(2,1)S(1)}, bf16[1,3...) fusion(bf16[3,5,162,384]{3,2,1,0:T(8,128)(2,1)S(1)} %select_max, ...), kind=kLoop, calls=%fused_computation.97 | loop fusion | bytes 13271040 | tf_op jit(solution)/shard_map/slice | solution.py:38
  39.3 1.3 %fusion.26 = (bf16[1,3,160,1152]{3,2,1,0:T(8,128)(2,1)S(1)}, bf16[1,3,160,1152]{3,2,1,0:T(8,128)(2,1)S(1)}, bf16[1,3,160,1152]{3,2,1,0:T(8,128)(2,1)S(1)}) fusion(bf16[3,1,160,384]{3,2,1,0:T(8,128)(2,1)S(1)} %collective-permute-done.2, bf16[1,3,160,384]{3,2,1,0:T(8,128)(2,1)S(1)} %fusion.43, bf16[1,3,160,384]{3,2,1,0:T(8,128)(2,1)S(1)} %collective-permute-done.1, ...), kind=kLoop, calls=%fused_computation.41 | loop fusion | flops 19906560 | bytes 7004160 | tf_op jit(solution)/shard_map/concatenate | solution.py:37
  40.5 0.8 fusion.55
  43.7 0.8 convolution_add_fusion.8
  45.3 0.8 convolution_add_fusion.6
  46.8 0.8 convolution_add_fusion.4
  47.6 0.8 convolution_add_fusion.3
  48.8 0.9 fusion.47
  49.8 1.4 %fusion.14 = bf16[480,384]{1,0:T(8,128)(2,1)S(1)} fusion(bf16[480,384]{1,0:T(8,128)(2,1)} %bitcast.75, bf16[384,384]{1,0:T(8,128)(2,1)S(1)} %copy-done.7, f32[384]{0:T(512)S(1)} %copy-done.10), kind=kOutput, calls=%fused_computation.31 | convolution fusion | flops 141926400 | bytes 1033728 | tf_op jit(solution)/shard_map/dot_general | solution.py:92
  51.2 32.2 %all-gather.2.cloned.1.call-done = bf16[1,12,160,384]{3,2,0,1:T(8,128)(2,1)} async-done(((bf16[1,3,160,384]{3,2,0,1:T(8,128)(2,1)}), bf16[1,12,160,384]{3,2,0,1:T(8,128)(2,1)}) %all-gather.2.cloned.1.call-update) | async-done | bytes 1474576 | tf_op jit(solution)/shard_map/all_gather | solution.py:100
  83.4 5.3 %multiply_reduce_fusion = (f32[480]{0:T(512)S(1)}, f32[480,1920]{1,0:T(8,128)}) fusion(bf16[480,384]{1,0:T(8,128)(2,1)S(1)} %fusion.14, bf16[1920,384]{1,0:T(8,128)(2,1)} %bitcast.79, bf16[384,384]{1,0:T(8,128)(2,1)S(1)} %copy-done), kind=kOutput, calls=%fused_computation.4 | convolution fusion | flops 1276599808 | bytes 5826432 | tf_op jit(solution)/shard_map/fqc,fkc->fqk/dot_general | solution.py:49
  88.7 2.2 %fusion.3 = bf16[1920,384]{1,0:T(8,128)(2,1)} fusion(bf16[1920,384]{1,0:T(8,128)(2,1)S(1)} %bitcast.80, bf16[384,384]{1,0:T(8,128)(2,1)S(1)} %copy-done.8, f32[384]{0:T(512)S(1)} %copy-done.11), kind=kOutput, calls=%fused_computation.9 | convolution fusion | flops 567705600 | bytes 3245568 | tf_op jit(solution)/shard_map/dot_general | solution.py:103
  92.4 3.5 %convolution_add_fusion.1 = f32[480,384]{1,0:T(8,128)S(1)} fusion(bf16[384,384]{1,0:T(8,128)(2,1)S(1)} %copy-done.9, bf16[1920,384]{1,0:T(8,128)(2,1)S(1)} %copy-done.13, f32[480,1920]{1,0:T(8,128)} %get-tuple-element.43, f32[480]{0:T(512)S(1)} %broadcast_maximum_fusion, f32[384]{0:T(512)S(1)} %copy-done.12, f32[480]{0:T(512)S(1)} %fusion.1), kind=kOutput, calls=%fused_computation.21 | convolution fusion | flops 852664320 | bytes 6198528 | tf_op jit(solution)/shard_map/dot_general | solution.py:107
  96.0 0.8 fusion.49
  (45 shorter events, 6.0 us)
Async XLA Ops:
  6.5 76.8 %copy-start = (bf16[384,384]{1,0:T(8,128)(2,1)S(1)}, bf16[384,384]{1,0:T(8,128)(2,1)}, u32[]{:S(2)}) copy-start(bf16[384,384]{1,0:T(8,128)(2,1)} %param.25) | copy-start | bytes 884740
  6.5 76.8 %all-gather.2.cloned.1.call-start = ((), (), s32[]{:S(2)}) async-start(), calls=%async_computation | async-start | bytes 1843200 | tf_op jit(solution)/shard_map/all_gather | solution.py:100
  9.1 13.9 %collective-permute-start.1 = (bf16[1,3,160,384]{3,2,1,0:T(8,128)(2,1)S(1)}, bf16[1,3,160,384]{3,2,1,0:T(8,128)(2,1)S(1)}, u32[]{:S(2)}, u32[]{:S(2)}) collective-permute-start(bf16[1,3,160,384]{3,2,1,0:T(8,128)(2,1)S(1)} %fusion.43), channel_id=1, source_target_pairs={{0,1},{1,2},{2,3},{4,5},{5,6},{6,7},{8,9},{9,10},{10,11},{12,13},{... | collective-permute-start | bytes 1105928 | tf_op jit(solution)/shard_map/ppermute | solution.py:10
  14.1 15.8 %collective-permute-start = (bf16[1,3,160,384]{3,2,1,0:T(8,128)(2,1)S(1)}, bf16[1,3,160,384]{3,2,1,0:T(8,128)(2,1)S(1)}, u32[]{:S(2)}, u32[]{:S(2)}) collective-permute-start(bf16[1,3,160,384]{3,2,1,0:T(8,128)(2,1)S(1)} %fusion.43), channel_id=1, source_target_pairs={{0,2},{1,3},{4,6},{5,7},{8,10},{9,11},{12,14},{13,15},{16,18},{17,... | collective-permute-start | bytes 1105928 | tf_op jit(solution)/shard_map/ppermute | solution.py:10
  29.9 6.6 %collective-permute-start.2 = (bf16[3,1,160,384]{3,2,1,0:T(8,128)(2,1)S(1)}, bf16[3,1,160,384]{3,2,1,0:T(8,128)(2,1)S(1)}, u32[]{:S(2)}, u32[]{:S(2)}) collective-permute-start(bf16[3,1,160,384]{3,2,1,0:T(8,128)(2,1)S(1)} %get-tuple-element.41), channel_id=1, source_target_pairs={{0,4},{4,8},{8,12},{1,5},{5,9},{9,13},{2,6},{6,10},{10,14},{3,7},{... | collective-permute-start | bytes 1105928 | tf_op jit(solution)/shard_map/ppermute | solution.py:20
  31.3 5.3 %collective-permute-start.3 = (bf16[3,1,160,384]{3,2,1,0:T(8,128)(2,1)S(1)}, bf16[3,1,160,384]{3,2,1,0:T(8,128)(2,1)S(1)}, u32[]{:S(2)}, u32[]{:S(2)}) collective-permute-start(bf16[3,1,160,384]{3,2,1,0:T(8,128)(2,1)S(1)} %get-tuple-element.40), channel_id=1, source_target_pairs={{4,0},{8,4},{12,8},{5,1},{9,5},{13,9},{6,2},{10,6},{14,10},{7,3},{... | collective-permute-start | bytes 1105928 | tf_op jit(solution)/shard_map/ppermute | solution.py:21
  47.6 1.0 copy-start.2
  47.6 1.0 copy-start.3
  47.6 1.2 %copy-start.4 = (f32[384]{0:T(512)S(1)}, f32[384]{0:T(512)}, u32[]{:S(2)}) copy-start(f32[384]{0:T(512)} %param.22) | copy-start | bytes 4612
  47.6 1.2 %copy-start.5 = (f32[384]{0:T(512)S(1)}, f32[384]{0:T(512)}, u32[]{:S(2)}) copy-start(f32[384]{0:T(512)} %param.21) | copy-start | bytes 4612
  48.4 1.4 %copy-start.7 = (bf16[384,384]{1,0:T(8,128)(2,1)S(1)}, bf16[384,384]{1,0:T(8,128)(2,1)}, u32[]{:S(2)}) copy-start(bf16[384,384]{1,0:T(8,128)(2,1)} %param.23) | copy-start | bytes 884740
  48.4 1.4 %copy-start.10 = (f32[384]{0:T(512)S(1)}, f32[384]{0:T(512)}, u32[]{:S(2)}) copy-start(f32[384]{0:T(512)} %param.24) | copy-start | bytes 4612
  83.3 5.4 %copy-start.6 = (bf16[1,12,160,384]{3,2,0,1:T(8,128)(2,1)S(1)}, bf16[1,12,160,384]{3,2,0,1:T(8,128)(2,1)}, u32[]{:S(2)}) copy-start(bf16[1,12,160,384]{3,2,0,1:T(8,128)(2,1)} %all-gather.2.cloned.1.call-done) | copy-start | bytes 4423684
  83.3 5.4 %copy-start.8 = (bf16[384,384]{1,0:T(8,128)(2,1)S(1)}, bf16[384,384]{1,0:T(8,128)(2,1)}, u32[]{:S(2)}) copy-start(bf16[384,384]{1,0:T(8,128)(2,1)} %param.26) | copy-start | bytes 884740
  83.3 5.4 %copy-start.11 = (f32[384]{0:T(512)S(1)}, f32[384]{0:T(512)}, u32[]{:S(2)}) copy-start(f32[384]{0:T(512)} %param.27) | copy-start | bytes 4612
  88.7 2.2 %copy-start.1 = (f32[480,1920]{1,0:T(8,128)S(1)}, f32[480,1920]{1,0:T(8,128)}, u32[]{:S(2)}) copy-start(f32[480,1920]{1,0:T(8,128)} %get-tuple-element.43) | copy-start | bytes 11059204
  90.9 1.0 copy-start.9
  90.9 1.0 copy-start.12
  90.9 1.5 %copy-start.13 = (bf16[1920,384]{1,0:T(8,128)(2,1)S(1)}, bf16[1920,384]{1,0:T(8,128)(2,1)}, u32[]{:S(2)}) copy-start(bf16[1920,384]{1,0:T(8,128)(2,1)} %fusion.3) | copy-start | bytes 4423684
Sparse Core Ops, SparseCore 0:
  49.9 33.4 all-gather.1
where the time goes:
time: 104 us
  waiting for transfers between devices  43.5 us (42%)
  matrix products  19.3 us (19%)
  between operations  13.7 us (13%)
  starting transfers between devices  12.1 us (12%)
  other arithmetic  9.02 us (9%)
  local copies, waits for them, and re-layouts  6.02 us (6%)
    all_gather x1, waiting for transfers between devices, shards(): lax.all_gather(normed, 'space', axis=1, tiled=True)  32.2 us
    ppermute x2, waiting for transfers between devices, from_behind(): lax.ppermute(value, axis, [(source, source + steps) for source in range(l...  11.2 us
    ppermute x2, starting transfers between devices, from_behind(): lax.ppermute(value, axis, [(source, source + steps) for source in range(l...  9.48 us
    dot_general x9, matrix products, causal_conv(): jnp.dot(joined, kernel, preferred_element_type=jnp.float32)  6.87 us
    dot_general x1, matrix products, absorb(): jnp.einsum('fqc,fkc->fqk', queries, key_rows, preferred_element_type=jnp....  5.34 us
    slice x1, local copies, waits for them, and re-layouts, causal_conv(): kernel = conv_weight[tap_t, tap_y].reshape(3 * channels, channels)  3.94 us
    dot_general x1, matrix products, shards(): jnp.dot(attended, out_weight, preferred_element_type=jnp.float32) + out_bias  3.54 us
    dot_general x1, matrix products, shards(): jnp.dot(source, value_weight, preferred_element_type=jnp.float32)  2.19 us
  transfers between devices with their start and end apart: 5, of which 4 were waited for; matrix products, arithmetic and copies ran while one was open for 5% of the time, Pallas kernels for 0%

commit v1 on v0

--- a/solution.py
+++ b/solution.py
@@ -2,6 +2,18 @@
 import jax.numpy as jnp
 from jax import lax
 from jax.sharding import PartitionSpec as P
+
+
+def gather_around(value, axis, dim):
+    ways, here, step = (lax.axis_size(axis), lax.axis_index(axis), value.shape[dim])
+    dims = [n * ways if d == dim else n for d, n in enumerate(value.shape)]
+    full = lax.dynamic_update_slice_in_dim(
+        jnp.zeros(dims, value.dtype), value, here * step, axis=dim
+    )
+    for far in range(1, ways):
+        value = lax.ppermute(value, axis, [(d, (d + 1) % ways) for d in range(ways)])
+        full = lax.dynamic_update_slice_in_dim(full, value, (here - far) % ways * step, axis=dim)
+    return full
 
 
 def from_behind(value, axis, steps):
@@ -97,7 +109,7 @@
         jnp.zeros((frame_count, query_count), jnp.float32),
         jnp.full((frame_count, query_count), -1e30, jnp.float32),
     )
-    source = lax.all_gather(normed, "space", axis=1, tiled=True).reshape(frame_count, -1, channels)
+    source = gather_around(normed, "space", 1).reshape(frame_count, -1, channels)
     key_rows = jnp.dot(source, key_weight, preferred_element_type=jnp.float32).astype(jnp.bfloat16)
     value_rows = (
         jnp.dot(source, value_weight, preferred_element_type=jnp.float32) + value_bias

time: 104 us -> 88.3 us (0.85)
  the two profiles are of different devices: /device:TPU:0 before, /device:TPU:22 now
where the time goes in v1:
time: 88.3 us; the launch traced here: 88.1 us
  waiting for transfers between devices  44.9 us (51%)
  matrix products  16.4 us (19%)
  starting transfers between devices  10.4 us (12%)
  other arithmetic  10.2 us (12%)
  local copies, waits for them, and re-layouts  5.76 us (7%)
    ppermute x2, waiting for transfers between devices, from_behind(): lax.ppermute(value, axis, [(source, source + steps) for source in range(l...  24.2 us
    ppermute x3, waiting for transfers between devices, gather_around(): lax.ppermute(value, axis, [(d, (d + 1) % ways) for d in range(ways)])  19.7 us
    dot_general x9, matrix products, causal_conv(): jnp.dot(joined, kernel, preferred_element_type=jnp.float32)  6.84 us
    ppermute x2, starting transfers between devices, from_behind(): lax.ppermute(value, axis, [(source, source + steps) for source in range(l...  4.78 us
    dot_general x1, matrix products, absorb(): jnp.einsum('fqk,fkc->fqc', weights, value_rows, preferred_element_type=jn...  4.16 us
    slice x1, local copies, waits for them, and re-layouts, causal_conv(): kernel = conv_weight[tap_t, tap_y].reshape(3 * channels, channels)  3.92 us
    dot_general x1, matrix products, absorb(): jnp.einsum('fqc,fkc->fqk', queries, key_rows, preferred_element_type=jnp....  3.88 us
    ppermute x1, starting transfers between devices, padded_2(): after = lax.ppermute(leading, axis, down)  3.64 us
  transfers between devices with their start and end apart: 7, of which 6 were waited for; matrix products, arithmetic and copies ran while one was open for 6% of the time, Pallas kernels for 0%

profile of v1, /device:TPU:22, one launch (start us, length us, event | category | flops | bytes accessed | tf_op | source)
XLA Modules:
  0.0 88.1 jit_solution(12622373397800710593)
XLA Ops:
  0.0 1.2 %fusion.33 = f32[3,160]{1,0:T(4,128)S(1)} fusion(bf16[1,3,160,384]{3,2,1,0:T(8,128)(2,1)} %param.16), kind=kLoop, calls=%fused_computation.72 | loop fusion | flops 552480 | bytes 370560 | tf_op jit(solution)/shard_map/reduce_sum | solution.py:39
  1.2 1.3 %fusion.41 = bf16[1,3,160,384]{3,2,1,0:T(8,128)(2,1)S(1)} fusion(bf16[1,3,160,384]{3,2,1,0:T(8,128)(2,1)} %param.16, f32[384]{0:T(512)} %param.18, f32[384]{0:T(512)} %param.17, f32[3,160]{1,0:T(4,128)S(1)} %add_rsqrt_fusion.1), kind=kLoop, calls=%fused_computation.80 | loop fusion | flops 1658880 | bytes 742272 | tf_op jit(solution)/shard_map/convert_element_type | solution.py:92
  2.6 1.3 %collective-permute-start = (bf16[1,3,160,384]{3,2,1,0:T(8,128)(2,1)S(1)}, bf16[1,3,160,384]{3,2,1,0:T(8,128)(2,1)S(1)}, u32[]{:S(2)}, u32[]{:S(2)}) collective-permute-start(bf16[1,3,160,384]{3,2,1,0:T(8,128)(2,1)S(1)} %fusion.41), channel_id=1, source_target_pairs={{0,2},{1,3},{4,6},{5,7},{8,10},{9,11},{12,14},{13,15},{16,18},{17,... | collective-permute-start | bytes 1105928 | tf_op jit(solution)/shard_map/ppermute | solution.py:22
  3.9 3.5 %collective-permute-start.1 = (bf16[1,3,160,384]{3,2,1,0:T(8,128)(2,1)S(1)}, bf16[1,3,160,384]{3,2,1,0:T(8,128)(2,1)S(1)}, u32[]{:S(2)}, u32[]{:S(2)}) collective-permute-start(bf16[1,3,160,384]{3,2,1,0:T(8,128)(2,1)S(1)} %fusion.41), channel_id=1, source_target_pairs={{0,1},{1,2},{2,3},{4,5},{5,6},{6,7},{8,9},{9,10},{10,11},{12,13},{... | collective-permute-start | bytes 1105928 | tf_op jit(solution)/shard_map/ppermute | solution.py:22
  7.4 9.5 %collective-permute-done = bf16[1,3,160,384]{3,2,1,0:T(8,128)(2,1)S(1)} collective-permute-done((bf16[1,3,160,384]{3,2,1,0:T(8,128)(2,1)S(1)}, bf16[1,3,160,384]{3,2,1,0:T(8,128)(2,1)S(1)}, u32[]{:S(2)}, u32[]{:S(2)}) %collective-permute-start) | collective-permute-done | bytes 368672 | tf_op jit(solution)/shard_map/ppermute | solution.py:22
  16.9 14.7 %collective-permute-done.1 = bf16[1,3,160,384]{3,2,1,0:T(8,128)(2,1)S(1)} collective-permute-done((bf16[1,3,160,384]{3,2,1,0:T(8,128)(2,1)S(1)}, bf16[1,3,160,384]{3,2,1,0:T(8,128)(2,1)S(1)}, u32[]{:S(2)}, u32[]{:S(2)}) %collective-permute-start.1) | collective-permute-done | bytes 368672 | tf_op jit(solution)/shard_map/ppermute | solution.py:22
  31.6 1.9 %collective-permute-start.2 = (bf16[3,1,160,384]{3,2,1,0:T(8,128)(2,1)S(1)}, bf16[3,1,160,384]{3,2,1,0:T(8,128)(2,1)S(1)}, u32[]{:S(2)}, u32[]{:S(2)}) collective-permute-start(bf16[3,1,160,384]{3,2,1,0:T(8,128)(2,1)S(1)} %get-tuple-element.43), channel_id=1, source_target_pairs={{0,4},{4,8},{8,12},{1,5},{5,9},{9,13},{2,6},{6,10},{10,14},{3,7},{... | collective-permute-start | bytes 1105928 | tf_op jit(solution)/shard_map/ppermute | solution.py:32
  33.6 3.6 %collective-permute-start.3 = (bf16[3,1,160,384]{3,2,1,0:T(8,128)(2,1)S(1)}, bf16[3,1,160,384]{3,2,1,0:T(8,128)(2,1)S(1)}, u32[]{:S(2)}, u32[]{:S(2)}) collective-permute-start(bf16[3,1,160,384]{3,2,1,0:T(8,128)(2,1)S(1)} %get-tuple-element.42), channel_id=1, source_target_pairs={{4,0},{8,4},{12,8},{5,1},{9,5},{13,9},{6,2},{10,6},{14,10},{7,3},{... | collective-permute-start | bytes 1105928 | tf_op jit(solution)/shard_map/ppermute | solution.py:33
  37.2 3.9 %fusion.49 = (bf16[1,1,3,384,384]{4,3,2,1,0:T(8,128)(2,1)S(1)}, bf16[1,1,3,384,384]{4,3,2,1,0:T(8,128)(2,1)S(1)}, bf16[1,1,3,384,384]{4,3,2,1,0:T(8,128)(2,1)S(1...) fusion(bf16[3,3,3,384,384]{4,3,2,1,0:T(8,128)(2,1)} %param.19), kind=kLoop, calls=%fused_computation.98 | loop fusion | bytes 15925248 | tf_op jit(solution)/shard_map/slice | solution.py:53
  41.1 1.1 %collective-permute-done.3 = bf16[3,1,160,384]{3,2,1,0:T(8,128)(2,1)S(1)} collective-permute-done((bf16[3,1,160,384]{3,2,1,0:T(8,128)(2,1)S(1)}, bf16[3,1,160,384]{3,2,1,0:T(8,128)(2,1)S(1)}, u32[]{:S(2)}, u32[]{:S(2)}) %collective-permute-start.3) | collective-permute-done | bytes 368672 | tf_op jit(solution)/shard_map/ppermute | solution.py:33
  42.2 1.5 %select_maximum_fusion = bf16[3,5,162,384]{3,2,1,0:T(8,128)(2,1)S(1)} fusion(bf16[3,1,160,384]{3,2,1,0:T(8,128)(2,1)S(1)} %collective-permute-done.3, bf16[3,1,160,384]{3,2,1,0:T(8,128)(2,1)S(1)} %collective-permute-done.2, bf16[1,3,160,384]{3,2,1,0:T(8,128)(2,1)S(1)} %fusion.41, bf16[1,3,160,384]{3,2,1,0:T(8,128)(2,1)S(1)} %collective-permute-done.1, ...), kind=kLoop, calls=%fused_computation.10 | loop fusion | flops 16796160 | bytes 3709440 | tf_op jit(solution)/shard_map/concatenate | solution.py:34
  43.8 1.1 %fusion.50 = (bf16[1,3,160,384]{3,2,1,0:T(8,128)(2,1)S(1)}, bf16[1,3,160,384]{3,2,1,0:T(8,128)(2,1)S(1)}, bf16[1,3,160,384]{3,2,1,0:T(8,128)(2,1)S(1)}, bf16[1,3...) fusion(bf16[3,5,162,384]{3,2,1,0:T(8,128)(2,1)S(1)} %select_max, ...), kind=kLoop, calls=%fused_computation.99 | loop fusion | bytes 13271040 | tf_op jit(solution)/shard_map/slice | solution.py:50
  44.9 1.3 %fusion.18 = (bf16[1,3,160,1152]{3,2,1,0:T(8,128)(2,1)S(1)}, bf16[1,3,160,1152]{3,2,1,0:T(8,128)(2,1)S(1)}, bf16[1,3,160,1152]{3,2,1,0:T(8,128)(2,1)S(1)}) fusion(bf16[3,1,160,384]{3,2,1,0:T(8,128)(2,1)S(1)} %collective-permute-done.2, bf16[1,3,160,384]{3,2,1,0:T(8,128)(2,1)S(1)} %fusion.41, bf16[1,3,160,384]{3,2,1,0:T(8,128)(2,1)S(1)} %collective-permute-done.1, ...), kind=kLoop, calls=%fused_computation.39 | loop fusion | flops 19906560 | bytes 7004160 | tf_op jit(solution)/shard_map/concatenate | solution.py:49
  51.5 0.8 convolution_add_fusion.5
  52.3 0.8 convolution_add_fusion.4
  53.1 0.8 convolution_add_fusion.3
  54.9 7.1 %collective-permute-done.4 = bf16[1,3,160,384]{3,2,1,0:T(8,128)(2,1)S(1)} collective-permute-done((bf16[1,3,160,384]{3,2,1,0:T(8,128)(2,1)S(1)}, bf16[1,3,160,384]{3,2,1,0:T(8,128)(2,1)S(1)}, u32[]{:S(2)}, u32[]{:S(2)}) %collective-permute-start.4) | collective-permute-done | bytes 368672 | tf_op jit(solution)/shard_map/ppermute | solution.py:14
  62.0 6.9 %collective-permute-done.5 = bf16[1,3,160,384]{3,2,1,0:T(8,128)(2,1)S(1)} collective-permute-done((bf16[1,3,160,384]{3,2,1,0:T(8,128)(2,1)S(1)}, bf16[1,3,160,384]{3,2,1,0:T(8,128)(2,1)S(1)}, u32[]{:S(2)}, u32[]{:S(2)}) %collective-permute-start.5) | collective-permute-done | bytes 368672 | tf_op jit(solution)/shard_map/ppermute | solution.py:14
  68.9 1.1 %fusion.14 = bf16[480,384]{1,0:T(8,128)(2,1)} fusion(bf16[480,384]{1,0:T(8,128)(2,1)S(1)} %bitcast.71, bf16[384,384]{1,0:T(8,128)(2,1)S(1)} %copy-done.7, f32[384]{0:T(512)S(1)} %copy-done.9), kind=kOutput, calls=%fused_computation.31 | convolution fusion | flops 141926400 | bytes 1033728 | tf_op jit(solution)/shard_map/dot_general | solution.py:104
  70.2 5.7 %collective-permute-done.6 = bf16[1,3,160,384]{3,2,1,0:T(8,128)(2,1)S(1)} collective-permute-done((bf16[1,3,160,384]{3,2,1,0:T(8,128)(2,1)S(1)}, bf16[1,3,160,384]{3,2,1,0:T(8,128)(2,1)S(1)}, u32[]{:S(2)}, u32[]{:S(2)}) %collective-permute-start.6) | collective-permute-done | bytes 368672 | tf_op jit(solution)/shard_map/ppermute | solution.py:14
  75.9 3.9 %multiply_reduce_fusion = (f32[480]{0:T(512)S(1)}, f32[480,1920]{1,0:T(8,128)}) fusion(bf16[480,384]{1,0:T(8,128)(2,1)S(1)} %copy-done.11, bf16[1920,384]{1,0:T(8,128)(2,1)S(1)} %bitcast.67, bf16[384,384]{1,0:T(8,128)(2,1)S(1)} %copy-done), kind=kOutput, calls=%fused_computation.4 | convolution fusion | flops 1276599808 | bytes 5826432 | tf_op jit(solution)/shard_map/fqc,fkc->fqk/dot_general | solution.py:61
  79.8 2.8 %fusion.1 = f32[480]{0:T(512)S(1)} fusion(f32[480,1920]{1,0:T(8,128)} %get-tuple-element.45, f32[480]{0:T(512)S(1)} %broadcast_maximum_fusion), kind=kLoop, calls=%fused_computation.5 | loop fusion | flops 2764320 | bytes 3690240 | tf_op jit(solution)/shard_map/reduce_sum | solution.py:69
  82.7 4.2 %fusion.30 = bf16[480,384]{1,0:T(8,128)(2,1)S(1)} fusion(bf16[1920,384]{1,0:T(8,128)(2,1)S(1)} %bitcast.68, bf16[384,384]{1,0:T(8,128)(2,1)S(1)} %copy-done.8, f32[384]{0:T(512)S(1)} %copy-done.10, f32[480,1920]{1,0:T(8,128)} %get-tuple-element.45, f32[480]{0:T(512)S(1)} %broadcast_maximum_fusion, f32[480]{0:T(512)S(1)} %fusion.1), kind=kOutput, calls=%fused_computation.69 | convolution fusion | flops 1278627840 | bytes 5829888 | tf_op jit(solution)/shard_map/fqk,fkc->fqc/dot_general | solution.py:67
  87.3 0.8 fusion.46
  (48 shorter events, 7.0 us)
Async XLA Ops:
  0.0 75.9 %copy-start = (bf16[384,384]{1,0:T(8,128)(2,1)S(1)}, bf16[384,384]{1,0:T(8,128)(2,1)}, u32[]{:S(2)}) copy-start(bf16[384,384]{1,0:T(8,128)(2,1)} %param.25) | copy-start | bytes 884740
  2.6 14.3 %collective-permute-start = (bf16[1,3,160,384]{3,2,1,0:T(8,128)(2,1)S(1)}, bf16[1,3,160,384]{3,2,1,0:T(8,128)(2,1)S(1)}, u32[]{:S(2)}, u32[]{:S(2)}) collective-permute-start(bf16[1,3,160,384]{3,2,1,0:T(8,128)(2,1)S(1)} %fusion.41), channel_id=1, source_target_pairs={{0,2},{1,3},{4,6},{5,7},{8,10},{9,11},{12,14},{13,15},{16,18},{17,... | collective-permute-start | bytes 1105928 | tf_op jit(solution)/shard_map/ppermute | solution.py:22
  3.9 27.7 %collective-permute-start.1 = (bf16[1,3,160,384]{3,2,1,0:T(8,128)(2,1)S(1)}, bf16[1,3,160,384]{3,2,1,0:T(8,128)(2,1)S(1)}, u32[]{:S(2)}, u32[]{:S(2)}) collective-permute-start(bf16[1,3,160,384]{3,2,1,0:T(8,128)(2,1)S(1)} %fusion.41), channel_id=1, source_target_pairs={{0,1},{1,2},{2,3},{4,5},{5,6},{6,7},{8,9},{9,10},{10,11},{12,13},{... | collective-permute-start | bytes 1105928 | tf_op jit(solution)/shard_map/ppermute | solution.py:22
  31.6 9.5 %collective-permute-start.2 = (bf16[3,1,160,384]{3,2,1,0:T(8,128)(2,1)S(1)}, bf16[3,1,160,384]{3,2,1,0:T(8,128)(2,1)S(1)}, u32[]{:S(2)}, u32[]{:S(2)}) collective-permute-start(bf16[3,1,160,384]{3,2,1,0:T(8,128)(2,1)S(1)} %get-tuple-element.43), channel_id=1, source_target_pairs={{0,4},{4,8},{8,12},{1,5},{5,9},{9,13},{2,6},{6,10},{10,14},{3,7},{... | collective-permute-start | bytes 1105928 | tf_op jit(solution)/shard_map/ppermute | solution.py:32
  33.6 8.7 %collective-permute-start.3 = (bf16[3,1,160,384]{3,2,1,0:T(8,128)(2,1)S(1)}, bf16[3,1,160,384]{3,2,1,0:T(8,128)(2,1)S(1)}, u32[]{:S(2)}, u32[]{:S(2)}) collective-permute-start(bf16[3,1,160,384]{3,2,1,0:T(8,128)(2,1)S(1)} %get-tuple-element.42), channel_id=1, source_target_pairs={{4,0},{8,4},{12,8},{5,1},{9,5},{13,9},{6,2},{10,6},{14,10},{7,3},{... | collective-permute-start | bytes 1105928 | tf_op jit(solution)/shard_map/ppermute | solution.py:33
  53.0 1.0 %copy-start.1 = (bf16[1,3,160,384]{3,2,1,0:T(8,128)(2,1)S(1)}, bf16[1,3,160,384]{3,2,1,0:T(8,128)(2,1)}, u32[]{:S(2)}) copy-start(bf16[1,3,160,384]{3,2,1,0:T(8,128)(2,1)} %param.15) | copy-start | bytes 1105924
  53.1 1.0 %copy-start.3 = (f32[384]{0:T(512)S(1)}, f32[384]{0:T(512)}, u32[]{:S(2)}) copy-start(f32[384]{0:T(512)} %param.20) | copy-start | bytes 4612
  53.8 0.7 copy-start.4
  53.9 0.7 copy-start.5
  54.0 14.9 %copy-start.7 = (bf16[384,384]{1,0:T(8,128)(2,1)S(1)}, bf16[384,384]{1,0:T(8,128)(2,1)}, u32[]{:S(2)}) copy-start(bf16[384,384]{1,0:T(8,128)(2,1)} %param.23) | copy-start | bytes 884740
  54.0 14.9 %copy-start.9 = (f32[384]{0:T(512)S(1)}, f32[384]{0:T(512)}, u32[]{:S(2)}) copy-start(f32[384]{0:T(512)} %param.24) | copy-start | bytes 4612
  54.8 7.2 %collective-permute-start.4 = (bf16[1,3,160,384]{3,2,1,0:T(8,128)(2,1)S(1)}, bf16[1,3,160,384]{3,2,1,0:T(8,128)(2,1)S(1)}, u32[]{:S(2)}, u32[]{:S(2)}) collective-permute-start(bf16[1,3,160,384]{3,2,1,0:T(8,128)(2,1)S(1)} %get-tuple-element.6), channel_id=1, source_target_pairs={{0,4},{4,8},{8,12},{12,0},{1,5},{5,9},{9,13},{13,1},{2,6},{6,10},{... | collective-permute-start | bytes 1105928 | tf_op jit(solution)/shard_map/ppermute | solution.py:14
  62.0 6.9 %collective-permute-start.5 = (bf16[1,3,160,384]{3,2,1,0:T(8,128)(2,1)S(1)}, bf16[1,3,160,384]{3,2,1,0:T(8,128)(2,1)S(1)}, u32[]{:S(2)}, u32[]{:S(2)}) collective-permute-start(bf16[1,3,160,384]{3,2,1,0:T(8,128)(2,1)S(1)} %collective-permute-done.4), channel_id=1, source_target_pairs={{0,4},{4,8},{8,12},{12,0},{1,5},{5,9},{9,13},{13,1},{2,6},{6,10},{... | collective-permute-start | bytes 1105928 | tf_op jit(solution)/shard_map/ppermute | solution.py:14
  68.9 6.9 %collective-permute-start.6 = (bf16[1,3,160,384]{3,2,1,0:T(8,128)(2,1)S(1)}, bf16[1,3,160,384]{3,2,1,0:T(8,128)(2,1)S(1)}, u32[]{:S(2)}, u32[]{:S(2)}) collective-permute-start(bf16[1,3,160,384]{3,2,1,0:T(8,128)(2,1)S(1)} %collective-permute-done.5), channel_id=1, source_target_pairs={{0,4},{4,8},{8,12},{12,0},{1,5},{5,9},{9,13},{13,1},{2,6},{6,10},{... | collective-permute-start | bytes 1105928 | tf_op jit(solution)/shard_map/ppermute | solution.py:14
  70.0 5.9 %copy-start.11 = (bf16[480,384]{1,0:T(8,128)(2,1)S(1)}, bf16[480,384]{1,0:T(8,128)(2,1)}, u32[]{:S(2)}) copy-start(bf16[480,384]{1,0:T(8,128)(2,1)} %fusion.14) | copy-start | bytes 1105924
  79.8 2.8 %copy-start.8 = (bf16[384,384]{1,0:T(8,128)(2,1)S(1)}, bf16[384,384]{1,0:T(8,128)(2,1)}, u32[]{:S(2)}) copy-start(bf16[384,384]{1,0:T(8,128)(2,1)} %param.26) | copy-start | bytes 884740
  79.8 2.8 %copy-start.10 = (f32[384]{0:T(512)S(1)}, f32[384]{0:T(512)}, u32[]{:S(2)}) copy-start(f32[384]{0:T(512)} %param.27) | copy-start | bytes 4612
  82.7 4.2 %copy-start.2 = (bf16[384,384]{1,0:T(8,128)(2,1)S(1)}, bf16[384,384]{1,0:T(8,128)(2,1)}, u32[]{:S(2)}) copy-start(bf16[384,384]{1,0:T(8,128)(2,1)} %param.28) | copy-start | bytes 884740
  82.7 4.2 %copy-start.6 = (f32[384]{0:T(512)S(1)}, f32[384]{0:T(512)}, u32[]{:S(2)}) copy-start(f32[384]{0:T(512)} %param.29) | copy-start | bytes 4612
